TPU v7x, 512 devices: a whole 4x4x16 slice. The times are simulated.
512 devices in a mesh: sp: 64 (over x_lo, z, core), hd: 8 (over y, x_hi).
Axes of the slice: x: 4 (x_hi: 2, x_lo: 2; x = x_hi * 2 + x_lo), y: 4, z: 16, core: 2. Of those that a mesh axis runs over, the one named last changes fastest.
Arguments:
- stream: bfloat16 [3, 8, 64, 5120], P(None, 'hd', 'sp'), may hold values from -6 to 6
- queries: bfloat16 [3, 8, 64, 5120], P(None, None, 'sp', 'hd'), may hold values from -40 to 40
- span_k: bfloat16 [3, 8, 64, 5120], P(None, None, 'sp', 'hd'), may hold values from -40 to 40
- span_v: bfloat16 [3, 8, 64, 5120], P(None, None, 'sp', 'hd'), may hold values from -6 to 6
- cache_k: bfloat16 [6144, 5120], P('sp', 'hd'), may hold values from -6 to 6
- cache_v: bfloat16 [6144, 5120], P('sp', 'hd'), may hold values from -6 to 6
- cache_age: int32 [6144], P('sp'), may hold values from 0 to 20, as said below
- history: int32 [1], replicated, may hold values from 1 to 20
- out_weight: bfloat16 [5120, 5120], P('hd', 'sp'), may hold values from -2 to 2
- attn_gate: float32 [5120], replicated, may hold values from 0.5 to 1.5
- head_shift: float32 [5120], replicated, may hold values from -3 to 3
- head_scale: float32 [5120], replicated, may hold values from -1.75 to 1.75
- head_weight: bfloat16 [5120, 64], replicated, may hold values from -0.078125 to 0.078125
- latent_cache: bfloat16 [2, 16, 128, 16], P(None, 'hd', 'sp'), may hold values from -6 to 6
- conv_weight: bfloat16 [432, 384], replicated, may hold values from -0.3125 to 0.3125
- rms_gain: float32 [384], replicated, may hold values from 0.25 to 1.75
Outputs:
- stream_out: bfloat16 [3, 8, 64, 5120], P(None, 'hd', 'sp')
- decoded: bfloat16 [3, 16, 128, 384], P(None, 'hd', 'sp')
Inputs may be any that keep to these rules, and one draw needn't show every extreme that they name: `cache_age`: 20 marks an empty cache slot. Among the 96 slots of each index of sp the live ones come first and number at least 24; some index of sp has all its slots live.
All inputs are finite; a program needn't handle non-finite values.
Results may differ from a plain program's by a relative error of at most 0.017.
Values may be sent and summed in bfloat16 or wider, within the bound.
No kernel may reach another device: no remote copies, remote signals or barrier semaphores. Data moves between devices by JAX's collectives and lax.ppermute only.
A program may use at most 64 MiB of HBM per device.

v0:
```python
import math
import jax
import jax.numpy as jnp
from jax import lax
from jax.sharding import PartitionSpec as P

HDIM = 128
LAT = 16
PATCH = 2


def padded_2(cells, sides, width):
    for axis, dim in sides:
        count = lax.axis_size(axis)
        ends = count - 1
        head = lax.slice_in_dim(cells, 0, width, axis=dim)
        tail = lax.slice_in_dim(cells, cells.shape[dim] - width, cells.shape[dim], axis=dim)
        cells = jnp.concatenate(
            [
                lax.ppermute(tail, axis, [(i, (i + 1) % count) for i in range(ends)]),
                cells,
                lax.ppermute(head, axis, [((i + 1) % count, i) for i in range(ends)]),
            ],
            axis=dim,
        )
    return cells


def head_partials(head_index, all_queries, all_keys, all_values, is_valid):
    offset = head_index * HDIM
    query_part = lax.dynamic_slice_in_dim(all_queries, offset, HDIM, 1)
    key_part = lax.dynamic_slice_in_dim(all_keys, offset, HDIM, 1)
    value_part = lax.dynamic_slice_in_dim(all_values, offset, HDIM, 1)
    scores = lax.dot_general(
        query_part, key_part, (((1,), (1,)), ((), ())), preferred_element_type=jnp.float32
    )
    scores = jnp.where(is_valid[None, :], scores * (1.0 / math.sqrt(HDIM)), -1e30)
    top_score = jnp.max(scores, axis=1)
    weights = jnp.exp(scores - top_score[:, None]).astype(jnp.bfloat16)
    weight_sum = jnp.sum(weights.astype(jnp.float32), axis=1)
    summed = jnp.dot(weights, value_part, preferred_element_type=jnp.float32)
    return (top_score, weight_sum, summed)


def settle(incoming):
    top_score, weight_sum, summed = incoming
    peak_score = jnp.max(top_score, axis=4, keepdims=True)
    factor = jnp.exp(top_score - peak_score)
    denominator = jnp.sum(weight_sum * factor, axis=4)
    numerator = jnp.sum(summed * factor[..., None], axis=4)
    return numerator / denominator[..., None]


def causal_conv(padded, frames, height, breadth, conv_weight, rms_gain):
    tap_list = []
    for step_t in range(3):
        for step_i in range(3):
            for step_j in range(3):
                tap_list.append(
                    padded[
                        step_t : step_t + frames,
                        step_i : step_i + height,
                        step_j : step_j + breadth,
                        :,
                    ]
                )
    patches = jnp.concatenate(tap_list, axis=-1)
    conv_out = jnp.dot(
        patches.reshape(-1, patches.shape[-1]), conv_weight, preferred_element_type=jnp.float32
    )
    mean_square = jnp.mean(conv_out * conv_out, axis=-1, keepdims=True)
    scaled = conv_out * lax.rsqrt(mean_square + 1e-06) * rms_gain
    return jax.nn.silu(scaled).astype(jnp.bfloat16).reshape(frames, height, breadth, -1)


def local(
    stream,
    queries,
    span_k,
    span_v,
    cache_k,
    cache_v,
    cache_age,
    history,
    out_weight,
    attn_gate,
    head_shift,
    head_scale,
    head_weight,
    latent_cache,
    conv_weight,
    rms_gain,
):
    frames = queries.shape[0]
    row_total = queries.shape[1]
    local_d = queries.shape[3]
    head_count = local_d // HDIM
    gathered = lax.all_gather(queries, "sp", axis=2, tiled=True)
    col_total = gathered.shape[2]
    all_queries = gathered.reshape(-1, local_d)
    all_keys = jnp.concatenate([cache_k, span_k.reshape(-1, local_d)], axis=0)
    all_values = jnp.concatenate([cache_v, span_v.reshape(-1, local_d)], axis=0)
    is_valid = jnp.concatenate([cache_age < history[0], jnp.ones((frames * row_total,), jnp.bool_)])

    def one_head(head_index):
        return head_partials(head_index, all_queries, all_keys, all_values, is_valid)

    top_score, weight_sum, summed = lax.map(one_head, jnp.arange(head_count, dtype=jnp.int32))
    top_parts = top_score.reshape(head_count, frames, row_total, col_total, 1)
    sum_parts = weight_sum.reshape(head_count, frames, row_total, col_total, 1)
    out_parts = summed.reshape(head_count, frames, row_total, col_total, 1, HDIM)
    attended_f = settle(
        (
            lax.all_to_all(top_parts, "sp", split_axis=3, concat_axis=4, tiled=True),
            lax.all_to_all(sum_parts, "sp", split_axis=3, concat_axis=4, tiled=True),
            lax.all_to_all(out_parts, "sp", split_axis=3, concat_axis=4, tiled=True),
        )
    )
    attended = (
        jnp.transpose(attended_f, (1, 2, 3, 0, 4))
        .reshape(frames, row_total, 1, local_d)
        .astype(jnp.bfloat16)
    )
    own_rows = attended.reshape(-1, local_d)
    partial_sum = jnp.dot(
        own_rows,
        lax.all_gather(out_weight, "sp", axis=1, tiled=True),
        preferred_element_type=jnp.float32,
    )
    projected = lax.psum_scatter(
        partial_sum.reshape(frames, row_total, 1, -1).astype(jnp.bfloat16),
        "hd",
        scatter_dimension=1,
        tiled=True,
    ).astype(jnp.float32)
    stream_out = (stream.astype(jnp.float32) + attn_gate * projected).astype(jnp.bfloat16)
    mixed_f = stream_out.astype(jnp.float32)
    centre_mean = jnp.mean(mixed_f, axis=-1, keepdims=True)
    centred = mixed_f - centre_mean
    variance = jnp.mean(centred * centred, axis=-1, keepdims=True)
    normed = (centred * lax.rsqrt(variance + 1e-06) * (1.0 + head_scale) + head_shift).astype(
        jnp.bfloat16
    )
    own_count = normed.shape[1]
    patch_values = jnp.dot(
        normed.reshape(-1, normed.shape[3]), head_weight, preferred_element_type=jnp.float32
    ).astype(jnp.bfloat16)
    patch_values = patch_values.reshape(frames, own_count, 1, PATCH, PATCH, LAT)
    latent = jnp.transpose(patch_values, (0, 1, 3, 2, 4, 5)).reshape(
        frames, own_count * PATCH, PATCH, LAT
    )
    sequence = jnp.concatenate([latent_cache, latent], axis=0)
    padded = padded_2(sequence, (("sp", 2), ("hd", 1)), 1)
    decoded = causal_conv(padded, frames, own_count * PATCH, PATCH, conv_weight, rms_gain)
    return (stream_out, decoded)


def solution(mesh):
    placed = (
        P(None, "hd", "sp", None),
        P(None, None, "sp", "hd"),
        P(None, None, "sp", "hd"),
        P(None, None, "sp", "hd"),
        P("sp", "hd"),
        P("sp", "hd"),
        P("sp"),
        P(),
        P("hd", "sp"),
        P(),
        P(),
        P(),
        P(),
        P(None, "hd", "sp", None),
        P(),
        P(),
    )
    return jax.shard_map(
        local,
        mesh=mesh,
        in_specs=placed,
        out_specs=(P(None, "hd", "sp", None), P(None, "hd", "sp", None)),
        check_vma=False,
    )
```

profile of v0, /device:TPU:6, one launch (start us, length us, event | category | flops | bytes accessed | tf_op | source)
XLA Modules:
  0.0 595.1 jit_solution(1144554674838404245)
XLA Ops:
  7.2 0.7 all-gather.3.cloned.1.call-update
  8.6 0.7 broadcast_compare_fusion
  9.3 1.0 pad_maximum_fusion
  10.3 125.3 %all-gather.3.cloned.1.call-done = bf16[3,8,64,640]{3,1,2,0:T(8,128)(2,1)} async-done(((bf16[3,8,1,640]{3,1,2,0:T(8,128)(2,1)}), bf16[3,8,64,640]{3,1,2,0:T(8,128)(2,1)}) %all-gather.3.cloned.1.call-update) | async-done | bytes 1966096 | tf_op jit(solution)/shard_map/all_gather | solution.py:98
  135.6 1.9 copy.44
  137.5 16.8 %while.14 = (s32[]{:T(128)}, f32[5,1536]{1,0:T(8,128)S(1)}, f32[5,1536]{1,0:T(8,128)S(1)}, f32[5,1536,128]{2,1,0:T(8,128)}, pred[120]{0:T(512)(128)(4,1)S(1)}, /...) while((s32[]{:T(128)}, f32[5,1536]{1,0:T(8,128)S(1)}, ...), condition=%wide.region_3.4_spmd, body=%wide.region_0.3_spmd.sunk | while | flops 96027648 | bytes 3530947 | solution.py:108
  137.5 0.6 dynamic_slice.30
  138.8 0.4 fusion.50
  139.2 1.2 fusion.51
  140.9 0.6 dynamic_slice.30
  142.1 0.4 fusion.50
  142.5 1.2 fusion.51
  144.3 0.6 dynamic_slice.30
  145.5 0.4 fusion.50
  145.9 1.2 fusion.51
  147.6 0.6 dynamic_slice.30
  148.9 0.4 fusion.50
  149.3 1.2 fusion.51
  151.0 0.6 dynamic_slice.30
  152.2 0.4 fusion.50
  152.6 1.2 fusion.51
  154.4 1.1 copy.46
  155.5 9.4 %all-to-all-start.1 = ((f32[5,3,8,64,1]{2,4,1,0,3:T(1,128)}), f32[5,3,8,64,1]{2,4,1,0,3:T(1,128)S(1)}, u32[]{:S(2)}, u32[]{:S(2)}) async-start(f32[5,3,8,64,1]{2,4,1,0,3:T(1,128)} %copy.46), calls=%async_computation.1 | async-start | bytes 983040 | tf_op jit(solution)/shard_map/all_to_all | solution.py:114
  165.0 1.1 copy.50
  166.1 27.0 %all-to-all-done.1 = f32[5,3,8,64,1]{2,4,1,0,3:T(1,128)S(1)} async-done(((f32[5,3,8,64,1]{2,4,1,0,3:T(1,128)}), f32[5,3,8,64,1]{2,4,1,0,3:T(1,128)S(1)}, u32[]{:S(2)}, u32[]{:S(2)}) %all-to-all-start.1) | async-done | bytes 30752 | tf_op jit(solution)/shard_map/all_to_all | solution.py:114
  193.1 7.9 %all-to-all-start.2 = ((f32[5,3,8,64,1]{2,4,1,0,3:T(1,128)}), f32[5,3,8,64,1]{2,4,1,0,3:T(1,128)S(1)}, u32[]{:S(2)}, u32[]{:S(2)}) async-start(f32[5,3,8,64,1]{2,4,1,0,3:T(1,128)} %copy.50), calls=%async_computation.2 | async-start | bytes 983040 | tf_op jit(solution)/shard_map/all_to_all | solution.py:115
  201.1 6.3 %copy.45 = f32[5,3,8,64,1,128]{5,2,1,0,4,3:T(8,128)} copy(f32[5,3,8,64,1,128]{5,3,2,1,0,4:T(8,128)} %bitcast.65) | data formatting | bytes 7864320 | tf_op jit(solution)/shard_map/reshape | solution.py:111
  207.4 21.8 %all-to-all-done.2 = f32[5,3,8,64,1]{2,4,1,0,3:T(1,128)S(1)} async-done(((f32[5,3,8,64,1]{2,4,1,0,3:T(1,128)}), f32[5,3,8,64,1]{2,4,1,0,3:T(1,128)S(1)}, u32[]{:S(2)}, u32[]{:S(2)}) %all-to-all-start.2) | async-done | bytes 30752 | tf_op jit(solution)/shard_map/all_to_all | solution.py:115
  229.2 8.1 %all-to-all-start = ((f32[5,3,8,64,1,128]{5,2,1,0,4,3:T(8,128)}), f32[5,3,8,64,1,128]{5,2,1,0,4,3:T(8,128)}, u32[]{:S(2)}, u32[]{:S(2)}) async-start(f32[5,3,8,64,1,128]{5,2,1,0,4,3:T(8,128)} %copy.45), calls=%async_computation | async-start | bytes 7864320 | tf_op jit(solution)/shard_map/all_to_all | solution.py:116
  237.4 0.7 all-gather.5.cloned.1.call-update
  238.1 0.4 copy.47
  238.6 0.4 reduce_max.18
  239.4 0.4 copy.51
  240.0 200.1 %all-to-all-done = f32[5,3,8,64,1,128]{5,2,1,0,4,3:T(8,128)} async-done(((f32[5,3,8,64,1,128]{5,2,1,0,4,3:T(8,128)}), f32[5,3,8,64,1,128]{5,2,1,0,4,3:T(8,128)}, u32[]{:S(2)}, u32[]{:S(2)}) %all-to-all-start) | async-done | bytes 3932192 | tf_op jit(solution)/shard_map/all_to_all | solution.py:116
  440.1 2.7 fusion.15
  442.9 20.5 %all-gather.5.cloned.1.call-done = bf16[640,5120]{0,1:T(8,128)(2,1)} async-done(((bf16[640,80]{0,1:T(8,128)(2,1)}), bf16[640,5120]{0,1:T(8,128)(2,1)}) %all-gather.5.cloned.1.call-update) | async-done | bytes 6553616 | tf_op jit(solution)/shard_map/all_gather | solution.py:127
  463.4 4.7 fusion.12
  468.1 0.9 copy.54
  469.1 1.3 dynamic-slice
  470.4 92.3 %all-reduce.4.cloned.1.call-done = bf16[3,8,1,5120]{3,0,2,1:T(4,128)(2,1)} async-done(((bf16[3,8,1,5120]{3,0,2,1:T(4,128)(2,1)}), bf16[3,8,1,5120]{3,0,2,1:T(4,128)(2,1)}) %all-reduce.4.cloned.1.call-update) | async-done | bytes 245776
  562.7 1.6 convert_reduce_fusion.1
  565.0 1.9 collective-permute-start
  567.0 5.8 collective-permute-start.1
  572.8 1.2 collective-permute-done.1
  574.2 4.9 collective-permute-start.2
  579.1 2.4 collective-permute-start.3
  581.6 5.4 collective-permute-done.3
  588.0 0.6 reshape.197
  (105 shorter events, 5.1 us)
Async XLA Ops:
  7.2 557.4 %copy-start = (bf16[5120,64]{0,1:T(8,128)(2,1)S(1)}, bf16[5120,64]{0,1:T(8,128)(2,1)}, u32[]{:S(2)}) copy-start(bf16[5120,64]{0,1:T(8,128)(2,1)} %param.30) | copy-start | bytes 1966084
  7.2 128.5 %all-gather.3.cloned.1.call-start = ((), (), s32[]{:S(2)}) async-start(), calls=%async_computation.3 | async-start | bytes 1996800 | tf_op jit(solution)/shard_map/all_gather | solution.py:98
  155.5 37.6 %all-to-all-start.1 = ((f32[5,3,8,64,1]{2,4,1,0,3:T(1,128)}), f32[5,3,8,64,1]{2,4,1,0,3:T(1,128)S(1)}, u32[]{:S(2)}, u32[]{:S(2)}) async-start(f32[5,3,8,64,1]{2,4,1,0,3:T(1,128)} %copy.46), calls=%async_computation.1 | async-start | bytes 983040 | tf_op jit(solution)/shard_map/all_to_all | solution.py:114
  193.1 36.1 %all-to-all-start.2 = ((f32[5,3,8,64,1]{2,4,1,0,3:T(1,128)}), f32[5,3,8,64,1]{2,4,1,0,3:T(1,128)S(1)}, u32[]{:S(2)}, u32[]{:S(2)}) async-start(f32[5,3,8,64,1]{2,4,1,0,3:T(1,128)} %copy.50), calls=%async_computation.2 | async-start | bytes 983040 | tf_op jit(solution)/shard_map/all_to_all | solution.py:115
  229.2 210.9 %all-to-all-start = ((f32[5,3,8,64,1,128]{5,2,1,0,4,3:T(8,128)}), f32[5,3,8,64,1,128]{5,2,1,0,4,3:T(8,128)}, u32[]{:S(2)}, u32[]{:S(2)}) async-start(f32[5,3,8,64,1,128]{5,2,1,0,4,3:T(8,128)} %copy.45), calls=%async_computation | async-start | bytes 7864320 | tf_op jit(solution)/shard_map/all_to_all | solution.py:116
  237.3 226.1 %all-gather.5.cloned.1.call-start = ((), (), s32[]{:S(2)}) async-start(), calls=%async_computation.4 | async-start | bytes 6656000 | tf_op jit(solution)/shard_map/all_gather | solution.py:127
  238.1 324.6 %all-reduce.4.cloned.1.call-start = ((), (), s32[]{:S(2)}) async-start(), calls=%async_computation.5 | async-start | bytes 655360
  442.8 26.2 %copy-start.7 = (bf16[2,2,2,16]{3,2,1,0:T(2,128)(2,1)S(1)}, bf16[2,2,2,16]{3,2,1,0:T(2,128)(2,1)}, u32[]{:S(2)}) copy-start(bf16[2,2,2,16]{3,2,1,0:T(2,128)(2,1)} %param.31) | copy-start | bytes 772
  442.8 27.5 %copy-start.5 = (f32[5120]{0:T(1024)S(1)}, f32[5120]{0:T(1024)}, u32[]{:S(2)}) copy-start(f32[5120]{0:T(1024)} %param.29) | copy-start | bytes 61444
  442.9 119.8 %copy-start.3 = (bf16[3,1,1,5120]{3,0,2,1:T(4,128)(2,1)S(1)}, bf16[3,1,1,5120]{3,0,2,1:T(4,128)(2,1)}, u32[]{:S(2)}) copy-start(bf16[3,1,1,5120]{3,0,2,1:T(4,128)(2,1)} %param.18) | copy-start | bytes 92164
  442.9 119.8 %copy-start.4 = (f32[5120]{0:T(1024)S(1)}, f32[5120]{0:T(1024)}, u32[]{:S(2)}) copy-start(f32[5120]{0:T(1024)} %param.27) | copy-start | bytes 61444
  442.9 121.7 %copy-start.8 = (f32[5120]{0:T(1024)S(1)}, f32[5120]{0:T(1024)}, u32[]{:S(2)}) copy-start(f32[5120]{0:T(1024)} %param.28) | copy-start | bytes 61444
  442.9 144.7 %copy-start.1 = (bf16[432,384]{1,0:T(8,128)(2,1)S(1)}, bf16[432,384]{1,0:T(8,128)(2,1)}, u32[]{:S(2)}) copy-start(bf16[432,384]{1,0:T(8,128)(2,1)} %param.32) | copy-start | bytes 995332
  442.9 145.0 %copy-start.6 = (f32[384]{0:T(512)S(1)}, f32[384]{0:T(512)}, u32[]{:S(2)}) copy-start(f32[384]{0:T(512)} %param.33) | copy-start | bytes 4612
  564.3 24.3 %copy-start.2 = (bf16[3,1,1,5120]{3,0,2,1:T(4,128)(2,1)}, bf16[3,1,1,5120]{3,0,2,1:T(4,128)(2,1)S(1)}, u32[]{:S(2)}) copy-start(bf16[3,1,1,5120]{3,0,2,1:T(4,128)(2,1)S(1)} %get-tuple-element.77) | copy-start | bytes 92164
  565.0 7.8 %collective-permute-start = (bf16[5,2,1,16]{3,2,1,0:T(2,128)(2,1)S(1)}, bf16[5,2,1,16]{3,2,1,0:T(2,128)(2,1)S(1)}, u32[]{:S(2)}, u32[]{:S(2)}) collective-permute-start(bf16[5,2,1,16]{3,2,1,0:T(2,128)(2,1)S(1)} %get-tuple-element.113), channel_id=1, source_target_pairs={{0,8},{8,16},{16,24},{24,32},{32,40},{40,48},{48,56},{56,64},{64,7... | collective-permute-start | bytes 968 | tf_op jit(solution)/shard_map/ppermute | solution.py:20
  567.0 7.1 %collective-permute-start.1 = (bf16[5,2,1,16]{3,2,1,0:T(2,128)(2,1)S(1)}, bf16[5,2,1,16]{3,2,1,0:T(2,128)(2,1)S(1)}, u32[]{:S(2)}, u32[]{:S(2)}) collective-permute-start(bf16[5,2,1,16]{3,2,1,0:T(2,128)(2,1)S(1)} %get-tuple-element.114), channel_id=1, source_target_pairs={{8,0},{16,8},{24,16},{32,24},{40,32},{48,40},{56,48},{64,56},{72,6... | collective-permute-start | bytes 968 | tf_op jit(solution)/shard_map/ppermute | solution.py:22
  574.2 7.5 %collective-permute-start.2 = (bf16[5,1,4,16]{3,2,1,0:T(4,128)(2,1)S(1)}, bf16[5,1,4,16]{3,2,1,0:T(4,128)(2,1)S(1)}, u32[]{:S(2)}, u32[]{:S(2)}) collective-permute-start(bf16[5,1,4,16]{3,2,1,0:T(4,128)(2,1)S(1)} %get-tuple-element.107), channel_id=1, source_target_pairs={{0,1},{1,2},{2,3},{3,4},{4,5},{5,6},{6,7},{8,9},{9,10},{10,11},{11... | collective-permute-start | bytes 1928 | tf_op jit(solution)/shard_map/ppermute | solution.py:20
  579.1 7.9 %collective-permute-start.3 = (bf16[5,1,4,16]{3,2,1,0:T(4,128)(2,1)S(1)}, bf16[5,1,4,16]{3,2,1,0:T(4,128)(2,1)S(1)}, u32[]{:S(2)}, u32[]{:S(2)}) collective-permute-start(bf16[5,1,4,16]{3,2,1,0:T(4,128)(2,1)S(1)} %get-tuple-element.106), channel_id=1, source_target_pairs={{1,0},{2,1},{3,2},{4,3},{5,4},{6,5},{7,6},{9,8},{10,9},{11,10},{12... | collective-permute-start | bytes 1928 | tf_op jit(solution)/shard_map/ppermute | solution.py:22
Sparse Core Ops, SparseCore 0:
  10.1 125.4 all-gather.2
  240.3 223.0 all-gather.4
  469.2 93.4 all-reduce.3
where the time goes:
time: 596 us; the launch traced here: 595 us
  waiting for transfers between devices  495 us (83%)
  starting transfers between devices  40.6 us (7%)
  local copies, waits for them, and re-layouts  20 us (3%)
  between operations  14.8 us (2%)
  matrix products  13.4 us (2%)
  other arithmetic  7.78 us (1%)
    all_to_all x1, waiting for transfers between devices, local(): lax.all_to_all(out_parts, 'sp', split_axis=3, concat_axis=4, tiled=True)  200 us
    all_gather x1, waiting for transfers between devices, local(): gathered = lax.all_gather(queries, 'sp', axis=2, tiled=True)  125 us
    unnamed x4, waiting for transfers between devices  93.7 us
    all_to_all x1, waiting for transfers between devices, local(): lax.all_to_all(top_parts, 'sp', split_axis=3, concat_axis=4, tiled=True)  27 us
    all_to_all x1, waiting for transfers between devices, local(): lax.all_to_all(sum_parts, 'sp', split_axis=3, concat_axis=4, tiled=True)  21.8 us
    all_gather x1, waiting for transfers between devices, local(): lax.all_gather(out_weight, 'sp', axis=1, tiled=True)  20.5 us
  transfers between devices with their start and end apart: 10, of which 8 were waited for; matrix products, arithmetic and copies ran while one was open for 3% of the time, Pallas kernels for 0%

commit v1 on v0

--- a/solution.py
+++ b/solution.py
@@ -95,7 +95,8 @@
     row_total = queries.shape[1]
     local_d = queries.shape[3]
     head_count = local_d // HDIM
-    gathered = lax.all_gather(queries, "sp", axis=2, tiled=True)
+    sent = jnp.stack([queries] * lax.axis_size("sp"))
+    gathered = jnp.concatenate(lax.all_to_all(sent, "sp", 0, 0), axis=2)
     col_total = gathered.shape[2]
     all_queries = gathered.reshape(-1, local_d)
     all_keys = jnp.concatenate([cache_k, span_k.reshape(-1, local_d)], axis=0)

time: 596 us -> 578 us (0.970)
  waiting for transfers between devices: 495 us -> 460 us
  starting transfers between devices: 40.6 us -> 56.8 us
    all_gather x1 -> x0, waiting for transfers between devices: 125 us -> none  [local(): gathered = lax.all_gather(queries, 'sp', axis=2, tiled=True)]
    all_to_all x0 -> x1, waiting for transfers between devices: none -> 90.1 us  [local(): gathered = jnp.concatenate(lax.all_to_all(sent, 'sp', 0, 0), axis=2)]
    all_to_all x0 -> x1, starting transfers between devices: none -> 17.4 us  [local(): gathered = jnp.concatenate(lax.all_to_all(sent, 'sp', 0, 0), axis=2)]
    unnamed x4 -> x3, waiting for transfers between devices: 93.7 us -> 93.3 us
  transfers between devices with their start and end apart: 10 -> 10, of which waited for: 8 -> 8; matrix products, arithmetic and copies ran while one was open for 3% -> 2% of each run, Pallas kernels for 0% -> 0%
where the time goes in v1:
time: 578 us; the launch traced here: 577 us
  waiting for transfers between devices  460 us (80%)
  starting transfers between devices  56.8 us (10%)
  local copies, waits for them, and re-layouts  22.3 us (4%)
  between operations  15.2 us (3%)
  matrix products  13.4 us (2%)
  other arithmetic  6.14 us (1%)
    all_to_all x1, waiting for transfers between devices, local(): lax.all_to_all(out_parts, 'sp', split_axis=3, concat_axis=4, tiled=True)  200 us
    unnamed x3, waiting for transfers between devices  93.3 us
    all_to_all x1, waiting for transfers between devices, local(): gathered = jnp.concatenate(lax.all_to_all(sent, 'sp', 0, 0), axis=2)  90.1 us
    all_to_all x1, waiting for transfers between devices, local(): lax.all_to_all(top_parts, 'sp', split_axis=3, concat_axis=4, tiled=True)  27 us
    all_to_all x1, waiting for transfers between devices, local(): lax.all_to_all(sum_parts, 'sp', split_axis=3, concat_axis=4, tiled=True)  21.8 us
    all_gather x1, waiting for transfers between devices, local(): lax.all_gather(out_weight, 'sp', axis=1, tiled=True)  20.5 us
    all_to_all x1, starting transfers between devices, local(): gathered = jnp.concatenate(lax.all_to_all(sent, 'sp', 0, 0), axis=2)  17.4 us
  transfers between devices with their start and end apart: 10, of which 8 were waited for; matrix products, arithmetic and copies ran while one was open for 2% of the time, Pallas kernels for 0%

profile of v1, /device:TPU:6, one launch (start us, length us, event | category | flops | bytes accessed | tf_op | source)
XLA Modules:
  0.0 576.9 jit_solution(8860743462386840622)
XLA Ops:
  7.2 2.2 stack.2
  9.5 17.4 %all-to-all-start = ((bf16[64,3,8,1,640]{4,2,1,3,0:T(8,128)(2,1)}), bf16[64,3,8,1,640]{4,2,1,3,0:T(8,128)(2,1)}, u32[]{:S(2)}, u32[]{:S(2)}) async-start(bf16[64,3,8,1,640]{4,2,1,3,0:T(8,128)(2,1)} %stack.2), calls=%async_computation | async-start | bytes 3932160 | tf_op jit(solution)/shard_map/all_to_all | solution.py:99
  27.7 90.1 %all-to-all-done = bf16[64,3,8,1,640]{4,2,1,3,0:T(8,128)(2,1)} async-done(((bf16[64,3,8,1,640]{4,2,1,3,0:T(8,128)(2,1)}), bf16[64,3,8,1,640]{4,2,1,3,0:T(8,128)(2,1)}, u32[]{:S(2)}, u32[]{:S(2)}) %all-to-all-start) | async-done | bytes 1966112 | tf_op jit(solution)/shard_map/all_to_all | solution.py:99
  117.8 1.9 copy.41
  119.7 16.9 %while.14 = (s32[]{:T(128)}, f32[5,1536]{1,0:T(8,128)S(1)}, f32[5,1536]{1,0:T(8,128)S(1)}, f32[5,1536,128]{2,1,0:T(8,128)}, pred[120]{0:T(512)(128)(4,1)S(1)}, /...) while((s32[]{:T(128)}, f32[5,1536]{1,0:T(8,128)S(1)}, ...), condition=%wide.region_3.4_spmd, body=%wide.region_0.3_spmd.sunk | while | flops 96027648 | bytes 3530947 | solution.py:109
  119.7 0.6 dynamic_slice.30
  120.9 0.4 fusion.50
  121.3 1.2 fusion.51
  123.1 0.6 dynamic_slice.30
  124.3 0.4 fusion.50
  124.7 1.2 fusion.51
  126.5 0.6 dynamic_slice.30
  127.7 0.4 fusion.50
  128.1 1.2 fusion.51
  129.8 0.6 dynamic_slice.30
  131.1 0.4 fusion.50
  131.5 1.2 fusion.51
  133.2 0.6 dynamic_slice.30
  134.4 0.4 fusion.50
  134.9 1.2 fusion.51
  136.7 1.1 copy.43
  137.7 8.3 %all-to-all-start.2 = ((f32[5,3,8,64,1]{2,4,1,0,3:T(1,128)}), f32[5,3,8,64,1]{2,4,1,0,3:T(1,128)S(1)}, u32[]{:S(2)}, u32[]{:S(2)}) async-start(f32[5,3,8,64,1]{2,4,1,0,3:T(1,128)} %copy.43), calls=%async_computation.2 | async-start | bytes 983040 | tf_op jit(solution)/shard_map/all_to_all | solution.py:115
  146.1 1.1 copy.47
  147.2 27.0 %all-to-all-done.2 = f32[5,3,8,64,1]{2,4,1,0,3:T(1,128)S(1)} async-done(((f32[5,3,8,64,1]{2,4,1,0,3:T(1,128)}), f32[5,3,8,64,1]{2,4,1,0,3:T(1,128)S(1)}, u32[]{:S(2)}, u32[]{:S(2)}) %all-to-all-start.2) | async-done | bytes 30752 | tf_op jit(solution)/shard_map/all_to_all | solution.py:115
  174.2 8.0 %all-to-all-start.3 = ((f32[5,3,8,64,1]{2,4,1,0,3:T(1,128)}), f32[5,3,8,64,1]{2,4,1,0,3:T(1,128)S(1)}, u32[]{:S(2)}, u32[]{:S(2)}) async-start(f32[5,3,8,64,1]{2,4,1,0,3:T(1,128)} %copy.47), calls=%async_computation.3 | async-start | bytes 983040 | tf_op jit(solution)/shard_map/all_to_all | solution.py:116
  182.1 6.3 %copy.42 = f32[5,3,8,64,1,128]{5,2,1,0,4,3:T(8,128)} copy(f32[5,3,8,64,1,128]{5,3,2,1,0,4:T(8,128)} %bitcast.68) | data formatting | bytes 7864320 | tf_op jit(solution)/shard_map/reshape | solution.py:112
  188.5 21.8 %all-to-all-done.3 = f32[5,3,8,64,1]{2,4,1,0,3:T(1,128)S(1)} async-done(((f32[5,3,8,64,1]{2,4,1,0,3:T(1,128)}), f32[5,3,8,64,1]{2,4,1,0,3:T(1,128)S(1)}, u32[]{:S(2)}, u32[]{:S(2)}) %all-to-all-start.3) | async-done | bytes 30752 | tf_op jit(solution)/shard_map/all_to_all | solution.py:116
  210.3 8.1 %all-to-all-start.1 = ((f32[5,3,8,64,1,128]{5,2,1,0,4,3:T(8,128)}), f32[5,3,8,64,1,128]{5,2,1,0,4,3:T(8,128)}, u32[]{:S(2)}, u32[]{:S(2)}) async-start(f32[5,3,8,64,1,128]{5,2,1,0,4,3:T(8,128)} %copy.42), calls=%async_computation.1 | async-start | bytes 7864320 | tf_op jit(solution)/shard_map/all_to_all | solution.py:117
  218.5 0.7 all-gather.2.cloned.1.call-update
  219.2 0.4 copy.44
  219.6 0.4 reduce_max.18
  220.5 0.4 copy.48
  221.1 200.2 %all-to-all-done.1 = f32[5,3,8,64,1,128]{5,2,1,0,4,3:T(8,128)} async-done(((f32[5,3,8,64,1,128]{5,2,1,0,4,3:T(8,128)}), f32[5,3,8,64,1,128]{5,2,1,0,4,3:T(8,128)}, u32[]{:S(2)}, u32[]{:S(2)}) %all-to-all-start.1) | async-done | bytes 3932192 | tf_op jit(solution)/shard_map/all_to_all | solution.py:117
  421.3 2.7 fusion.15
  424.1 20.5 %all-gather.2.cloned.1.call-done = bf16[640,5120]{0,1:T(8,128)(2,1)} async-done(((bf16[640,80]{0,1:T(8,128)(2,1)}), bf16[640,5120]{0,1:T(8,128)(2,1)}) %all-gather.2.cloned.1.call-update) | async-done | bytes 6553616 | tf_op jit(solution)/shard_map/all_gather | solution.py:128
  444.6 4.7 fusion.12
  449.3 1.0 copy.51
  450.3 1.3 dynamic-slice
  451.6 92.6 %all-reduce.4.cloned.1.call-done = bf16[3,8,1,5120]{3,0,2,1:T(4,128)(2,1)} async-done(((bf16[3,8,1,5120]{3,0,2,1:T(4,128)(2,1)}), bf16[3,8,1,5120]{3,0,2,1:T(4,128)(2,1)}) %all-reduce.4.cloned.1.call-update) | async-done | bytes 245776
  544.2 1.6 convert_reduce_fusion.1
  546.0 0.3 convolution_convert_fusion
  546.5 1.9 collective-permute-start
  548.4 5.8 collective-permute-start.1
  554.3 1.2 collective-permute-done.1
  555.6 4.9 collective-permute-start.2
  560.6 2.4 collective-permute-start.3
  563.1 5.4 collective-permute-done.3
  569.5 0.6 reshape.200
  (115 shorter events, 4.8 us)
Async XLA Ops:
  7.2 538.9 %copy-start = (bf16[5120,64]{0,1:T(8,128)(2,1)S(1)}, bf16[5120,64]{0,1:T(8,128)(2,1)}, u32[]{:S(2)}) copy-start(bf16[5120,64]{0,1:T(8,128)(2,1)} %param.30) | copy-start | bytes 1966084
  7.2 20.4 %copy-start.13 = (s32[96]{0:T(128)S(1)}, s32[96]{0:T(128)}, u32[]{:S(2)}) copy-start(s32[96]{0:T(128)} %param.24) | copy-start | bytes 1156
  7.2 20.4 %copy-start.6 = (bf16[3,8,1,640]{3,1,2,0:T(8,128)(2,1)S(1)}, bf16[3,8,1,640]{3,1,2,0:T(8,128)(2,1)}, u32[]{:S(2)}) copy-start(bf16[3,8,1,640]{3,1,2,0:T(8,128)(2,1)} %param.20) | copy-start | bytes 92164
  7.2 20.4 %copy-start.7 = (bf16[3,8,1,640]{3,1,2,0:T(8,128)(2,1)S(1)}, bf16[3,8,1,640]{3,1,2,0:T(8,128)(2,1)}, u32[]{:S(2)}) copy-start(bf16[3,8,1,640]{3,1,2,0:T(8,128)(2,1)} %param.21) | copy-start | bytes 92164
  7.2 20.4 %copy-start.3 = (bf16[96,640]{1,0:T(8,128)(2,1)S(1)}, bf16[96,640]{1,0:T(8,128)(2,1)}, u32[]{:S(2)}) copy-start(bf16[96,640]{1,0:T(8,128)(2,1)} %param.22) | copy-start | bytes 368644
  7.2 20.4 %copy-start.4 = (bf16[96,640]{1,0:T(8,128)(2,1)S(1)}, bf16[96,640]{1,0:T(8,128)(2,1)}, u32[]{:S(2)}) copy-start(bf16[96,640]{1,0:T(8,128)(2,1)} %param.23) | copy-start | bytes 368644
  9.5 108.3 %all-to-all-start = ((bf16[64,3,8,1,640]{4,2,1,3,0:T(8,128)(2,1)}), bf16[64,3,8,1,640]{4,2,1,3,0:T(8,128)(2,1)}, u32[]{:S(2)}, u32[]{:S(2)}) async-start(bf16[64,3,8,1,640]{4,2,1,3,0:T(8,128)(2,1)} %stack.2), calls=%async_computation | async-start | bytes 3932160 | tf_op jit(solution)/shard_map/all_to_all | solution.py:99
  137.7 36.4 %all-to-all-start.2 = ((f32[5,3,8,64,1]{2,4,1,0,3:T(1,128)}), f32[5,3,8,64,1]{2,4,1,0,3:T(1,128)S(1)}, u32[]{:S(2)}, u32[]{:S(2)}) async-start(f32[5,3,8,64,1]{2,4,1,0,3:T(1,128)} %copy.43), calls=%async_computation.2 | async-start | bytes 983040 | tf_op jit(solution)/shard_map/all_to_all | solution.py:115
  174.2 36.1 %all-to-all-start.3 = ((f32[5,3,8,64,1]{2,4,1,0,3:T(1,128)}), f32[5,3,8,64,1]{2,4,1,0,3:T(1,128)S(1)}, u32[]{:S(2)}, u32[]{:S(2)}) async-start(f32[5,3,8,64,1]{2,4,1,0,3:T(1,128)} %copy.47), calls=%async_computation.3 | async-start | bytes 983040 | tf_op jit(solution)/shard_map/all_to_all | solution.py:116
  210.3 211.0 %all-to-all-start.1 = ((f32[5,3,8,64,1,128]{5,2,1,0,4,3:T(8,128)}), f32[5,3,8,64,1,128]{5,2,1,0,4,3:T(8,128)}, u32[]{:S(2)}, u32[]{:S(2)}) async-start(f32[5,3,8,64,1,128]{5,2,1,0,4,3:T(8,128)} %copy.42), calls=%async_computation.1 | async-start | bytes 7864320 | tf_op jit(solution)/shard_map/all_to_all | solution.py:117
  218.4 226.2 %all-gather.2.cloned.1.call-start = ((), (), s32[]{:S(2)}) async-start(), calls=%async_computation.4 | async-start | bytes 6656000 | tf_op jit(solution)/shard_map/all_gather | solution.py:128
  219.2 325.0 %all-reduce.4.cloned.1.call-start = ((), (), s32[]{:S(2)}) async-start(), calls=%async_computation.5 | async-start | bytes 655360
  424.0 26.2 %copy-start.11 = (bf16[2,2,2,16]{3,2,1,0:T(2,128)(2,1)S(1)}, bf16[2,2,2,16]{3,2,1,0:T(2,128)(2,1)}, u32[]{:S(2)}) copy-start(bf16[2,2,2,16]{3,2,1,0:T(2,128)(2,1)} %param.31) | copy-start | bytes 772
  424.0 27.5 %copy-start.9 = (f32[5120]{0:T(1024)S(1)}, f32[5120]{0:T(1024)}, u32[]{:S(2)}) copy-start(f32[5120]{0:T(1024)} %param.29) | copy-start | bytes 61444
  424.1 120.1 %copy-start.5 = (bf16[3,1,1,5120]{3,0,2,1:T(4,128)(2,1)S(1)}, bf16[3,1,1,5120]{3,0,2,1:T(4,128)(2,1)}, u32[]{:S(2)}) copy-start(bf16[3,1,1,5120]{3,0,2,1:T(4,128)(2,1)} %param.18) | copy-start | bytes 92164
  424.1 120.1 %copy-start.8 = (f32[5120]{0:T(1024)S(1)}, f32[5120]{0:T(1024)}, u32[]{:S(2)}) copy-start(f32[5120]{0:T(1024)} %param.27) | copy-start | bytes 61444
  424.1 122.0 %copy-start.12 = (f32[5120]{0:T(1024)S(1)}, f32[5120]{0:T(1024)}, u32[]{:S(2)}) copy-start(f32[5120]{0:T(1024)} %param.28) | copy-start | bytes 61444
  424.1 145.0 %copy-start.1 = (bf16[432,384]{1,0:T(8,128)(2,1)S(1)}, bf16[432,384]{1,0:T(8,128)(2,1)}, u32[]{:S(2)}) copy-start(bf16[432,384]{1,0:T(8,128)(2,1)} %param.32) | copy-start | bytes 995332
  424.1 145.3 %copy-start.10 = (f32[384]{0:T(512)S(1)}, f32[384]{0:T(512)}, u32[]{:S(2)}) copy-start(f32[384]{0:T(512)} %param.33) | copy-start | bytes 4612
  545.8 24.3 %copy-start.2 = (bf16[3,1,1,5120]{3,0,2,1:T(4,128)(2,1)}, bf16[3,1,1,5120]{3,0,2,1:T(4,128)(2,1)S(1)}, u32[]{:S(2)}) copy-start(bf16[3,1,1,5120]{3,0,2,1:T(4,128)(2,1)S(1)} %get-tuple-element.77) | copy-start | bytes 92164
  546.5 7.8 %collective-permute-start = (bf16[5,2,1,16]{3,2,1,0:T(2,128)(2,1)S(1)}, bf16[5,2,1,16]{3,2,1,0:T(2,128)(2,1)S(1)}, u32[]{:S(2)}, u32[]{:S(2)}) collective-permute-start(bf16[5,2,1,16]{3,2,1,0:T(2,128)(2,1)S(1)} %get-tuple-element.113), channel_id=1, source_target_pairs={{0,8},{8,16},{16,24},{24,32},{32,40},{40,48},{48,56},{56,64},{64,7... | collective-permute-start | bytes 968 | tf_op jit(solution)/shard_map/ppermute | solution.py:20
  548.4 7.1 %collective-permute-start.1 = (bf16[5,2,1,16]{3,2,1,0:T(2,128)(2,1)S(1)}, bf16[5,2,1,16]{3,2,1,0:T(2,128)(2,1)S(1)}, u32[]{:S(2)}, u32[]{:S(2)}) collective-permute-start(bf16[5,2,1,16]{3,2,1,0:T(2,128)(2,1)S(1)} %get-tuple-element.114), channel_id=1, source_target_pairs={{8,0},{16,8},{24,16},{32,24},{40,32},{48,40},{56,48},{64,56},{72,6... | collective-permute-start | bytes 968 | tf_op jit(solution)/shard_map/ppermute | solution.py:22
  555.6 7.5 %collective-permute-start.2 = (bf16[5,1,4,16]{3,2,1,0:T(4,128)(2,1)S(1)}, bf16[5,1,4,16]{3,2,1,0:T(4,128)(2,1)S(1)}, u32[]{:S(2)}, u32[]{:S(2)}) collective-permute-start(bf16[5,1,4,16]{3,2,1,0:T(4,128)(2,1)S(1)} %get-tuple-element.107), channel_id=1, source_target_pairs={{0,1},{1,2},{2,3},{3,4},{4,5},{5,6},{6,7},{8,9},{9,10},{10,11},{11... | collective-permute-start | bytes 1928 | tf_op jit(solution)/shard_map/ppermute | solution.py:20
  560.6 7.9 %collective-permute-start.3 = (bf16[5,1,4,16]{3,2,1,0:T(4,128)(2,1)S(1)}, bf16[5,1,4,16]{3,2,1,0:T(4,128)(2,1)S(1)}, u32[]{:S(2)}, u32[]{:S(2)}) collective-permute-start(bf16[5,1,4,16]{3,2,1,0:T(4,128)(2,1)S(1)} %get-tuple-element.106), channel_id=1, source_target_pairs={{1,0},{2,1},{3,2},{4,3},{5,4},{6,5},{7,6},{9,8},{10,9},{11,10},{12... | collective-permute-start | bytes 1928 | tf_op jit(solution)/shard_map/ppermute | solution.py:22
Sparse Core Ops, SparseCore 0:
  221.4 223.1 all-gather.1
  450.4 93.7 all-reduce.3
